TPU v7x, 32 devices: a whole 2x2x4 slice. The times are simulated.
32 devices in a mesh: dp: 8 (over z, x), fsdp: 4 (over y, core).
Axes of the slice: x: 2, y: 2, z: 4, core: 2. Of those that a mesh axis runs over, the one named last changes fastest.
Arguments:
- tokens: bfloat16 [16384, 1024], P(('dp', 'fsdp')), may hold values from -6 to 6
- segment_ids: int32 [16384], P(('dp', 'fsdp')), may hold values from 0 to 16383, as said below
- pad_mask: int32 [16384], P(('dp', 'fsdp')), may hold values 0 or 1
- cotangent: bfloat16 [16384, 1024], P(('dp', 'fsdp')), may hold values from -6 to 6
- w_qkv: bfloat16 [1024, 3072], P(('dp', 'fsdp')), may hold values from -0.1875 to 0.1875
- b_query: bfloat16 [1024], P(('dp', 'fsdp')), may hold values from -3 to 3
- b_value: bfloat16 [1024], P(('dp', 'fsdp')), may hold values from -3 to 3
- w_out: bfloat16 [1024, 1024], P(('dp', 'fsdp')), may hold values from -0.75 to 0.75
- b_out: bfloat16 [1024], P(('dp', 'fsdp')), may hold values from -3 to 3
- gain_attn: bfloat16 [1024], P(('dp', 'fsdp')), may hold values from 0.25 to 1.75
- shift_attn: bfloat16 [1024], P(('dp', 'fsdp')), may hold values from -3 to 3
- w_up: bfloat16 [1024, 4096], P(('dp', 'fsdp')), may hold values from -0.1875 to 0.1875
- b_up: bfloat16 [4096], P(('dp', 'fsdp')), may hold values from -3 to 3
- w_down: bfloat16 [4096, 1024], P(('dp', 'fsdp')), may hold values from -0.09375 to 0.09375
- b_down: bfloat16 [1024], P(('dp', 'fsdp')), may hold values from -3 to 3
- gain_ffn: bfloat16 [1024], P(('dp', 'fsdp')), may hold values from 0.25 to 1.75
- shift_ffn: bfloat16 [1024], P(('dp', 'fsdp')), may hold values from -3 to 3
Outputs:
- layer_output: bfloat16 [16384, 1024], P(('dp', 'fsdp'))
- grad_tokens: float32 [16384, 1024], P(('dp', 'fsdp'))
- grad_w_qkv: float32 [1024, 3072], P(('dp', 'fsdp'))
- grad_b_query: float32 [1024], P(('dp', 'fsdp'))
- grad_b_value: float32 [1024], P(('dp', 'fsdp'))
- grad_w_out: float32 [1024, 1024], P(('dp', 'fsdp'))
- grad_b_out: float32 [1024], P(('dp', 'fsdp'))
- grad_gain_attn: float32 [1024], P(('dp', 'fsdp'))
- grad_shift_attn: float32 [1024], P(('dp', 'fsdp'))
- grad_w_up: float32 [1024, 4096], P(('dp', 'fsdp'))
- grad_b_up: float32 [4096], P(('dp', 'fsdp'))
- grad_w_down: float32 [4096, 1024], P(('dp', 'fsdp'))
- grad_b_down: float32 [1024], P(('dp', 'fsdp'))
- grad_gain_ffn: float32 [1024], P(('dp', 'fsdp'))
- grad_shift_ffn: float32 [1024], P(('dp', 'fsdp'))
Inputs may be any that keep to these rules, and one draw needn't show every extreme that they name: `segment_ids`: each token's id is the index of the first token of its segment; ids never fall along the tokens; tokens with equal ids lie in one aligned block of 256 tokens.
All inputs are finite; a program needn't handle non-finite values. No bound on the sum of `pad_mask` on one device may be relied on, other than what follows from the above.
Results may differ from a plain program's by a relative error of at most 0.012.
Values may be sent and summed in bfloat16 or wider, within the bound.
A program may use at most 192 MiB of HBM per device.

v0:
```python
import jax
import jax.numpy as jnp
from jax import lax
from jax.sharding import PartitionSpec as P

HEADS = 16
BLOCK = 512


NEG_FILL = -1e30
EPSILON = 1e-05


def layer_norm(hidden, gain, shift):
    center = hidden - jnp.mean(hidden, -1, keepdims=True)
    spread = jnp.mean(center * center, -1, keepdims=True)
    return center * lax.rsqrt(spread + EPSILON) * gain + shift


def gelu_exact(values_in):
    return jax.nn.gelu(values_in, approximate=False)


def rows_dot(left, right):
    return lax.dot_general(
        left, right, (((0,), (0,)), ((), ())), preferred_element_type=jnp.float32
    )


def back_dot(left, right):
    return lax.dot_general(
        left, right, (((1,), (1,)), ((), ())), preferred_element_type=jnp.float32
    )


def masked_scores(queries, key_rows, seg_block, pad_block):
    scale = float(queries.shape[-1]) ** (-0.5)
    scores = (
        jnp.einsum("qhd,khd->hqk", queries, key_rows, preferred_element_type=jnp.float32) * scale
    )
    span = seg_block.shape[0]
    diagonal = lax.broadcasted_iota(jnp.int32, (span, span), 0) == lax.broadcasted_iota(
        jnp.int32, (span, span), 1
    )
    allowed = (seg_block[:, None] == seg_block[None, :]) & ((pad_block[None, :] == 1) | diagonal)
    return jnp.where(allowed[None], scores, NEG_FILL)


def attend_forward(pieces):
    queries, key_rows, value_rows, seg_block, pad_block = pieces
    scores = masked_scores(queries, key_rows, seg_block, pad_block)
    row_top = jnp.max(scores, -1, keepdims=True)
    row_total = jnp.sum(jnp.exp(scores - row_top), -1, keepdims=True)
    log_total = row_top + jnp.log(row_total)
    weights = jnp.exp(scores - log_total).astype(jnp.bfloat16)
    context = jnp.einsum("hqk,khd->qhd", weights, value_rows, preferred_element_type=jnp.float32)
    return (context.astype(jnp.bfloat16), log_total)


def attend_backward(pieces):
    queries, key_rows, value_rows, context_grad, log_total, seg_block, pad_block = pieces
    scale = float(queries.shape[-1]) ** (-0.5)
    scores = masked_scores(queries, key_rows, seg_block, pad_block)
    probabilities = jnp.exp(scores - log_total)
    value_grad = jnp.einsum(
        "hqk,qhd->khd",
        probabilities.astype(jnp.bfloat16),
        context_grad,
        preferred_element_type=jnp.float32,
    )
    prob_grad = jnp.einsum(
        "qhd,khd->hqk", context_grad, value_rows, preferred_element_type=jnp.float32
    )
    row_inner = jnp.sum(probabilities * prob_grad, -1, keepdims=True)
    score_grad = (probabilities * (prob_grad - row_inner)).astype(jnp.bfloat16)
    query_grad = (
        jnp.einsum("hqk,khd->qhd", score_grad, key_rows, preferred_element_type=jnp.float32) * scale
    )
    key_grad = (
        jnp.einsum("hqk,qhd->khd", score_grad, queries, preferred_element_type=jnp.float32) * scale
    )
    return (
        query_grad.astype(jnp.bfloat16),
        key_grad.astype(jnp.bfloat16),
        value_grad.astype(jnp.bfloat16),
    )


def body(
    tokens,
    segment_ids,
    pad_mask,
    cotangent,
    w_qkv,
    b_query,
    b_value,
    w_out,
    b_out,
    gain_attn,
    shift_attn,
    w_up,
    b_up,
    w_down,
    b_down,
    gain_ffn,
    shift_ffn,
):
    gathered = (
        lax.all_gather(w_qkv, ("dp", "fsdp"), axis=0, tiled=True),
        lax.all_gather(b_query, ("dp", "fsdp"), axis=0, tiled=True),
        lax.all_gather(b_value, ("dp", "fsdp"), axis=0, tiled=True),
        lax.all_gather(w_out, ("dp", "fsdp"), axis=0, tiled=True),
        lax.all_gather(b_out, ("dp", "fsdp"), axis=0, tiled=True),
        lax.all_gather(gain_attn, ("dp", "fsdp"), axis=0, tiled=True),
        lax.all_gather(shift_attn, ("dp", "fsdp"), axis=0, tiled=True),
        lax.all_gather(w_up, ("dp", "fsdp"), axis=0, tiled=True),
        lax.all_gather(b_up, ("dp", "fsdp"), axis=0, tiled=True),
        lax.all_gather(w_down, ("dp", "fsdp"), axis=0, tiled=True),
        lax.all_gather(b_down, ("dp", "fsdp"), axis=0, tiled=True),
        lax.all_gather(gain_ffn, ("dp", "fsdp"), axis=0, tiled=True),
        lax.all_gather(shift_ffn, ("dp", "fsdp"), axis=0, tiled=True),
    )
    (
        qkv_full,
        query_bias,
        value_bias,
        out_full,
        out_bias,
        gain_one,
        shift_one,
        up_full,
        up_bias,
        down_full,
        down_bias,
        gain_two,
        shift_two,
    ) = gathered
    row_count, model_width = tokens.shape
    head_count = HEADS
    head_dim = model_width // head_count
    block_count = row_count // BLOCK

    def split_heads(array):
        return array.reshape(block_count, BLOCK, head_count, head_dim)

    seg_blocks = segment_ids.reshape(block_count, BLOCK)
    pad_blocks = pad_mask.reshape(block_count, BLOCK)
    projected = jnp.dot(tokens, qkv_full, preferred_element_type=jnp.float32)
    queries = (projected[:, :model_width] + query_bias.astype(jnp.float32)).astype(jnp.bfloat16)
    key_rows = projected[:, model_width : 2 * model_width].astype(jnp.bfloat16)
    value_rows = (projected[:, 2 * model_width :] + value_bias.astype(jnp.float32)).astype(
        jnp.bfloat16
    )
    context, log_totals = lax.map(
        attend_forward,
        (
            split_heads(queries),
            split_heads(key_rows),
            split_heads(value_rows),
            seg_blocks,
            pad_blocks,
        ),
    )
    context = context.reshape(row_count, model_width)
    residual_one = (
        tokens.astype(jnp.float32)
        + jnp.dot(context, out_full, preferred_element_type=jnp.float32)
        + out_bias.astype(jnp.float32)
    )
    normed, norm_one_back = jax.vjp(
        layer_norm, residual_one, gain_one.astype(jnp.float32), shift_one.astype(jnp.float32)
    )
    normed_low = normed.astype(jnp.bfloat16)
    upward = jnp.dot(normed_low, up_full, preferred_element_type=jnp.float32) + up_bias.astype(
        jnp.float32
    )
    active, gelu_back = jax.vjp(gelu_exact, upward)
    active_low = active.astype(jnp.bfloat16)
    residual_two = (
        normed
        + jnp.dot(active_low, down_full, preferred_element_type=jnp.float32)
        + down_bias.astype(jnp.float32)
    )
    result, norm_two_back = jax.vjp(
        layer_norm, residual_two, gain_two.astype(jnp.float32), shift_two.astype(jnp.float32)
    )
    qkv_use, out_use, up_use, down_use = (
        lax.all_gather(w_qkv, ("dp", "fsdp"), axis=0, tiled=True),
        lax.all_gather(w_out, ("dp", "fsdp"), axis=0, tiled=True),
        lax.all_gather(w_up, ("dp", "fsdp"), axis=0, tiled=True),
        lax.all_gather(w_down, ("dp", "fsdp"), axis=0, tiled=True),
    )
    grad_two, grad_gain_two, grad_shift_two = norm_two_back(cotangent.astype(jnp.float32))
    branch_grad = grad_two.astype(jnp.bfloat16)
    grad_down = rows_dot(active_low, branch_grad)
    grad_down_bias = jnp.sum(branch_grad.astype(jnp.float32), 0)
    (up_grad,) = gelu_back(back_dot(branch_grad, down_use))
    up_grad_low = up_grad.astype(jnp.bfloat16)
    grad_up = rows_dot(normed_low, up_grad_low)
    grad_up_bias = jnp.sum(up_grad_low.astype(jnp.float32), 0)
    normed_grad = grad_two + back_dot(up_grad_low, up_use)
    grad_one, grad_gain_one, grad_shift_one = norm_one_back(normed_grad)
    attn_grad = grad_one.astype(jnp.bfloat16)
    grad_out = rows_dot(context, attn_grad)
    grad_out_bias = jnp.sum(attn_grad.astype(jnp.float32), 0)
    context_grad = back_dot(attn_grad, out_use).astype(jnp.bfloat16)
    query_grad, key_grad, value_grad = lax.map(
        attend_backward,
        (
            split_heads(queries),
            split_heads(key_rows),
            split_heads(value_rows),
            split_heads(context_grad),
            log_totals,
            seg_blocks,
            pad_blocks,
        ),
    )
    query_grad = query_grad.reshape(row_count, model_width)
    key_grad = key_grad.reshape(row_count, model_width)
    value_grad = value_grad.reshape(row_count, model_width)
    qkv_grad = jnp.concatenate([query_grad, key_grad, value_grad], axis=1)
    grad_qkv = rows_dot(tokens, qkv_grad)
    grad_query_bias = jnp.sum(query_grad.astype(jnp.float32), 0)
    grad_value_bias = jnp.sum(value_grad.astype(jnp.float32), 0)
    grad_tokens = grad_one + back_dot(qkv_grad, qkv_use)
    every_shard = (
        lax.psum_scatter(grad_qkv, ("dp", "fsdp"), scatter_dimension=0, tiled=True),
        lax.psum_scatter(grad_query_bias, ("dp", "fsdp"), scatter_dimension=0, tiled=True),
        lax.psum_scatter(grad_value_bias, ("dp", "fsdp"), scatter_dimension=0, tiled=True),
        lax.psum_scatter(grad_out, ("dp", "fsdp"), scatter_dimension=0, tiled=True),
        lax.psum_scatter(grad_out_bias, ("dp", "fsdp"), scatter_dimension=0, tiled=True),
        lax.psum_scatter(grad_gain_one, ("dp", "fsdp"), scatter_dimension=0, tiled=True),
        lax.psum_scatter(grad_shift_one, ("dp", "fsdp"), scatter_dimension=0, tiled=True),
        lax.psum_scatter(grad_up, ("dp", "fsdp"), scatter_dimension=0, tiled=True),
        lax.psum_scatter(grad_up_bias, ("dp", "fsdp"), scatter_dimension=0, tiled=True),
        lax.psum_scatter(grad_down, ("dp", "fsdp"), scatter_dimension=0, tiled=True),
        lax.psum_scatter(grad_down_bias, ("dp", "fsdp"), scatter_dimension=0, tiled=True),
        lax.psum_scatter(grad_gain_two, ("dp", "fsdp"), scatter_dimension=0, tiled=True),
        lax.psum_scatter(grad_shift_two, ("dp", "fsdp"), scatter_dimension=0, tiled=True),
    )
    (
        shard_qkv,
        shard_query,
        shard_value,
        shard_out,
        shard_out_bias,
        shard_gain_one,
        shard_shift_one,
        shard_up,
        shard_up_bias,
        shard_down,
        shard_down_bias,
        shard_gain_two,
        shard_shift_two,
    ) = every_shard
    return (
        result.astype(jnp.bfloat16),
        grad_tokens,
        shard_qkv,
        shard_query,
        shard_value,
        shard_out,
        shard_out_bias,
        shard_gain_one,
        shard_shift_one,
        shard_up,
        shard_up_bias,
        shard_down,
        shard_down_bias,
        shard_gain_two,
        shard_shift_two,
    )


def solution(mesh):
    placed = (
        P(("dp", "fsdp"), None),
        P(("dp", "fsdp")),
        P(("dp", "fsdp")),
        P(("dp", "fsdp"), None),
        P(("dp", "fsdp"), None),
        P(("dp", "fsdp")),
        P(("dp", "fsdp")),
        P(("dp", "fsdp"), None),
        P(("dp", "fsdp")),
        P(("dp", "fsdp")),
        P(("dp", "fsdp")),
        P(("dp", "fsdp"), None),
        P(("dp", "fsdp")),
        P(("dp", "fsdp"), None),
        P(("dp", "fsdp")),
        P(("dp", "fsdp")),
        P(("dp", "fsdp")),
    )
    return jax.shard_map(
        body,
        mesh=mesh,
        in_specs=placed,
        out_specs=(
            P(("dp", "fsdp"), None),
            P(("dp", "fsdp"), None),
            P(("dp", "fsdp"), None),
            P(("dp", "fsdp")),
            P(("dp", "fsdp")),
            P(("dp", "fsdp"), None),
            P(("dp", "fsdp")),
            P(("dp", "fsdp")),
            P(("dp", "fsdp")),
            P(("dp", "fsdp"), None),
            P(("dp", "fsdp")),
            P(("dp", "fsdp"), None),
            P(("dp", "fsdp")),
            P(("dp", "fsdp")),
            P(("dp", "fsdp")),
        ),
        check_vma=False,
    )
```

profile of v0, /device:TPU:0, one launch (start us, length us, event | category | flops | bytes accessed | tf_op | source)
XLA Modules:
  0.0 1017.9 jit_solution(11506093260011062171)
XLA Ops:
  7.2 0.7 all-gather.6.cloned.1.call-update
  8.0 0.7 all-gather.8.cloned.1.call-update
  8.7 0.7 all-gather.10.cloned.1.call-update
  10.0 0.8 dynamic-update-slice
  10.9 0.8 dynamic-update-slice.1
  11.7 0.8 dynamic-update-slice.2
  12.6 0.8 dynamic-update-slice.4
  13.4 0.8 dynamic-update-slice.3
  14.2 0.8 dynamic-update-slice.5
  15.1 0.8 dynamic-update-slice.7
  15.9 0.8 dynamic-update-slice.6
  16.7 42.4 %all-reduce.18 = (bf16[1024]{0:T(1024)(128)(2,1)S(1)}, bf16[1024]{0:T(1024)(128)(2,1)S(1)}, bf16[1024]{0:T(1024)(128)(2,1)S(1)}, bf16[1024]{0:T(1024)(128)(2,1)S...) all-reduce(bf16[1024]{0:T(1024)(128)(2,1)S(1)} %dynamic-update-slic, ...), channel_id=1, replica_groups=mesh['dp'=8,'fsdp'=4] {'dp','fsdp'}, use_global_device_ids=true, to_apply=%add | all-reduce | flops 8192 | bytes 32768
  59.2 41.0 %all-gather = bf16[32,1,128]{2,1,0:T(2,128)(2,1)S(1)} all-gather(bf16[1,1,128]{2,1,0:T(2,128)(2,1)} %bitcast.69), channel_id=1, replica_groups=mesh['dp'=8,'fsdp'=4] {'dp','fsdp'}, dimensions={0}, use_global_device_ids=true | all-gather | bytes 8448 | tf_op jit(solution)/shard_map/all_gather | solution.py:117
  100.3 0.7 broadcast_compare_fusion
  100.9 1.0 fusion.16
  102.0 5.8 fusion.36
  107.8 1.1 slice.23
  108.9 0.6 fusion.12
  109.6 0.5 copy.54
  110.7 1.5 copy.56
  112.2 7.4 fusion
  119.6 9.2 exponential_reduce_fusion
  128.8 9.1 convolution_convert_fusion.1
  137.9 2.9 all-gather.8.cloned.1.call-done
  140.8 3.5 fusion.34
  144.7 74.9 %all-gather.10.cloned.1.call-done = bf16[1024,4096]{1,0:T(8,128)(2,1)} async-done(((bf16[32,4096]{1,0:T(8,128)(2,1)}), bf16[1024,4096]{1,0:T(8,128)(2,1)}) %all-gather.10.cloned.1.call-update) | async-done | bytes 8388624 | tf_op jit(solution)/shard_map/all_gather | solution.py:116
  219.6 27.7 %multiply_convert_fusion.1 = (bf16[512,4096]{1,0:T(8,128)(2,1)}, f32[512,4096]{1,0:T(8,128)}, f32[512,4096]{1,0:T(8,128)}) fusion(f32[4096]{0:T(1024)S(1)} %bitcast.67, bf16[1024,4096]{1,0:T(8,128)(2,1)} %all-gather.10.cloned.1.call-done, f32[512,1024]{1,0:T(8,128)S(1)} %get-tuple-element.158, f32[1024]{0:T(1024)S(1)} %convert_element_type.126, ...), kind=kOutput, calls=%fused_computation.11 | convolution fusion | flops 4436000768 | bytes 31485952 | tf_op jit(solution)/shard_map/dot_general | solution.py:174
  247.4 50.7 %all-gather.12.cloned.1.call-done = bf16[4096,1024]{1,0:T(8,128)(2,1)} async-done(((bf16[128,1024]{1,0:T(8,128)(2,1)}), bf16[4096,1024]{1,0:T(8,128)(2,1)}) %all-gather.12.cloned.1.call-update) | async-done | bytes 8388624 | tf_op jit(solution)/shard_map/all_gather | solution.py:118
  298.1 8.5 fusion.35
  306.9 0.8 fusion.11
  307.7 1.9 fusion.32
  309.9 13.8 %convert_reduce_fusion = (f32[4096]{0:T(1024)S(1)}, bf16[512,4096]{1,0:T(8,128)(2,1)S(1)}) fusion(f32[512,4096]{1,0:T(8,128)} %get-tuple-element.151, f32[512,4096]{1,0:T(8,128)} %get-tuple-element.159, f32[4096]{0:T(1024)S(1)} %bitcast.68, bf16[512,1024]{1,0:T(8,128)(2,1)S(1)} %get-tuple-element.141, bf16[4096,1024]{1,0:T(8,128)(2,1)} %all-gather.12.cloned.1.call-done), kind=kOutput, calls=%fused_computation.9 | convolution fusion | flops 4330614784 | bytes 30441472 | tf_op jit(solution)/shard_map/dot_general | solution.py:31
  323.7 9.1 multiply_reduce_fusion.1
  332.9 0.7 fusion.31
  333.6 1.3 copy-done.2
  335.2 1.0 copy-done.10
  336.2 3.2 fusion.37
  339.5 4.2 convolution_convert_fusion.2
  343.7 2.4 copy.58
  346.1 12.3 %multiply_reduce_fusion = (f32[16,512]{1,0:T(8,128)S(1)}, f32[16,512,512]{1,2,0:T(8,128)}) fusion(f32[16,512,512]{1,2,0:T(8,128)} %get-tuple-element.156, f32[16,512]{1,0:T(8,128)S(1)} %log_add_fusion, pred[512,512]{0,1:T(8,128)(4,1)S(1)} %fusion.16, bf16[512,16,64]{0,2,1:T(8,128)(2,1)} %bitcast.59, bf16[512,16,64]{0,2,1:T(8,128)(2,1)} %bitcast.58), kind=kOutput, calls=%fused_computation.1 | convolution fusion | flops 557834240 | bytes 35979264 | tf_op jit(solution)/shard_map/while/body/eval_jaxpr/qhd,khd->hqk/dot_general | solution.py:71
  358.4 12.3 %multiply_convert_fusion = bf16[16,512,512]{1,2,0:T(8,128)(2,1)S(1)} fusion(f32[16,512,512]{1,2,0:T(8,128)} %get-tuple-element.164, f32[16,512,512]{1,2,0:T(8,128)} %get-tuple-element.156, f32[16,512]{1,0:T(8,128)S(1)} %get-tuple-element.163, f32[16,512]{1,0:T(8,128)S(1)} %log_add_fusion, pred[512,512]{0,1:T(8,128)(4,1)S(1)} %fusion.16), kind=kLoop, calls=%fused_computation | loop fusion | flops 25165824 | bytes 42270720 | tf_op jit(solution)/shard_map/while/body/eval_jaxpr/convert_element_type | solution.py:75
  370.7 2.6 multiply_convert_fusion.2
  373.4 1.5 convert_reduce_fusion.5
  375.0 8.3 convert_reduce_fusion.4
  383.3 1.0 copy-done.13
  384.3 10.3 %convolution_bitcast_fusion = f32[1024,3072]{0,1:T(8,128)} fusion(bf16[512,1024]{1,0:T(8,128)(2,1)S(1)} %copy-done.11, bf16[512,1024]{0,1:T(8,128)(2,1)S(1)} %bitcast.70, bf16[512,1024]{0,1:T(8,128)(2,1)S(1)} %bitcast.63, bf16[512,1024]{0,1:T(8,128)(2,1)S(1)} %bitcast.61), kind=kOutput, calls=%fused_computation.25 | convolution fusion | flops 3230662656 | bytes 16777216 | tf_op jit(solution)/shard_map/dot_general | solution.py:25
  394.6 12.6 %copy.67 = f32[1024,3072]{1,0:T(8,128)} copy(f32[1024,3072]{0,1:T(8,128)} %convolution_bitcast_fusion) | data formatting | bytes 25165824
  407.2 10.4 %fusion.27 = f32[1024,4096]{1,0:T(8,128)} fusion(bf16[512,4096]{1,0:T(8,128)(2,1)} %copy-done.14, f32[512,1024]{1,0:T(8,128)S(1)} %get-tuple-element.158, f32[1024]{0:T(1024)S(1)} %convert_element_type.126, f32[1024]{0:T(1024)S(1)} %convert_element_type.125, f32[512]{0:T(512)S(1)} %fusion.19, f32[512]{0:T(512)S(1)} %broadcast_multiply_fusion.1), kind=kOutput, calls=%fused_computation.84 | convolution fusion | flops 4297588736 | bytes 23080960 | tf_op jit(solution)/shard_map/dot_general | solution.py:25
  417.8 1.1 copy-done.9
  418.9 10.4 %fusion.38 = f32[4096,1024]{1,0:T(8,128)} fusion(bf16[512,4096]{1,0:T(8,128)(2,1)} %get-tuple-element.150, bf16[512,1024]{1,0:T(8,128)(2,1)S(1)} %copy-done.9), kind=kOutput, calls=%fused_computation.92 | convolution fusion | flops 4294967296 | bytes 22020096 | tf_op jit(solution)/shard_map/dot_general | solution.py:25
  429.5 41.2 %all-reduce.17 = (f32[1024]{0:T(1024)S(1)}, f32[1024]{0:T(1024)S(1)}, f32[1024]{0:T(1024)S(1)}, f32[1024]{0:T(1024)S(1)}, f32[1024]{0:T(1024)S(1)}, /*index=5*/f...) all-reduce(f32[1024]{0:T(1024)S(1)} %reduce_sum.220, ...), channel_id=3, replica_groups=mesh['dp'=8,'fsdp'=4] {'dp','fsdp'}, use_global_device_ids=true, to_apply=%region_13.14.clone | all-reduce | flops 12288 | bytes 98304
  470.7 0.6 dynamic-slice.3
  471.3 0.6 dynamic-slice.4
  471.8 0.6 dynamic-slice.5
  472.4 0.6 dynamic-slice.6
  473.0 0.6 dynamic-slice.7
  473.6 0.6 dynamic-slice.9
  474.2 0.6 dynamic-slice.10
  474.8 0.6 dynamic-slice.11
  475.3 0.6 dynamic-slice.8
  475.9 8.3 add_add_fusion.4
  484.2 154.0 %reduce-scatter.13.cloned.1.call-done = f32[32,3072]{1,0:T(8,128)} async-done(((f32[1024,3072]{1,0:T(8,128)}), f32[32,3072]{1,0:T(8,128)}) %reduce-scatter.13.cloned.1.call-update) | async-done | bytes 393232
  638.2 185.0 %reduce-scatter.9.cloned.1.call-done = f32[32,4096]{1,0:T(8,128)} async-done(((f32[1024,4096]{1,0:T(8,128)}), f32[32,4096]{1,0:T(8,128)}) %reduce-scatter.9.cloned.1.call-update) | async-done | bytes 524304 | tf_op jit(solution)/shard_map/reduce_scatter | solution.py:235
  823.2 187.5 %reduce-scatter.11.cloned.1.call-done = f32[128,1024]{1,0:T(8,128)} async-done(((f32[4096,1024]{1,0:T(8,128)}), f32[128,1024]{1,0:T(8,128)}) %reduce-scatter.11.cloned.1.call-update) | async-done | bytes 524304 | tf_op jit(solution)/shard_map/reduce_scatter | solution.py:237
  (74 shorter events, 3.1 us)
Async XLA Ops:
  7.2 94.8 %all-gather.6.cloned.1.call-start = ((), (), s32[]{:S(2)}) async-start(), calls=%async_computation.4 | async-start | bytes 6488064 | tf_op jit(solution)/shard_map/all_gather | solution.py:109
  7.9 132.9 %all-gather.8.cloned.1.call-start = ((), (), s32[]{:S(2)}) async-start(), calls=%async_computation.5 | async-start | bytes 2162688 | tf_op jit(solution)/shard_map/all_gather | solution.py:112
  8.7 211.0 %all-gather.10.cloned.1.call-start = ((), (), s32[]{:S(2)}) async-start(), calls=%async_computation.6 | async-start | bytes 8650752 | tf_op jit(solution)/shard_map/all_gather | solution.py:116
  9.4 288.7 %all-gather.12.cloned.1.call-start = ((), (), s32[]{:S(2)}) async-start(), calls=%async_computation.7 | async-start | bytes 8650752 | tf_op jit(solution)/shard_map/all_gather | solution.py:118
  10.0 474.3 %reduce-scatter.7.cloned.1.call-start = ((), (), s32[]{:S(2)}) async-start(), calls=%async_computation.8 | async-start | bytes 4325376 | tf_op jit(solution)/shard_map/reduce_scatter | solution.py:231
  110.1 18.7 %copy-start.4 = (bf16[512,1024]{0,1:T(8,128)(2,1)}, bf16[512,1024]{0,1:T(8,128)(2,1)S(1)}, u32[]{:S(2)}) copy-start(bf16[512,1024]{0,1:T(8,128)(2,1)S(1)} %copy.54) | copy-start | bytes 3145732
  112.2 7.4 copy-start
  298.1 8.9 copy-start.6
  309.9 13.8 %copy-start.8 = (bf16[512,1024]{1,0:T(8,128)(2,1)}, bf16[512,1024]{1,0:T(8,128)(2,1)S(1)}, u32[]{:S(2)}) copy-start(bf16[512,1024]{1,0:T(8,128)(2,1)S(1)} %get-tuple-element.141) | copy-start | bytes 3145732
  323.7 9.1 copy-start.14
  332.9 3.3 copy-start.12
  333.6 1.3 copy-start.2
  335.2 1.0 copy-start.10
  339.4 298.8 %reduce-scatter.13.cloned.1.call-start = ((), (), s32[]{:S(2)}) async-start(), calls=%async_computation.11 | async-start | bytes 12976128
  370.7 2.6 copy-start.1
  373.4 10.0 copy-start.7
  373.4 1.6 copy-start.5
  375.0 9.3 copy-start.11
  383.3 1.0 copy-start.13
  407.2 416.0 %reduce-scatter.9.cloned.1.call-start = ((), (), s32[]{:S(2)}) async-start(), calls=%async_computation.9 | async-start | bytes 17301504 | tf_op jit(solution)/shard_map/reduce_scatter | solution.py:235
  417.7 1.2 copy-start.9
  417.7 593.0 %reduce-scatter.11.cloned.1.call-start = ((), (), s32[]{:S(2)}) async-start(), calls=%async_computation.10 | async-start | bytes 17301504 | tf_op jit(solution)/shard_map/reduce_scatter | solution.py:237
  429.3 46.6 %copy-start.3 = (f32[512,1024]{1,0:T(8,128)S(1)}, f32[512,1024]{1,0:T(8,128)}, u32[]{:S(2)}) copy-start(f32[512,1024]{1,0:T(8,128)} %copy-done.2) | copy-start | bytes 6291460
Sparse Core Ops, SparseCore 0:
  10.9 72.2 all-gather.5
  86.0 54.7 all-gather.7
  143.7 75.9 all-gather.9
  222.3 75.6 all-gather.11
  339.5 141.3 reduce-scatter.6
  487.4 150.7 reduce-scatter.12
  641.1 182.0 reduce-scatter.8
  826.1 184.6 reduce-scatter.10
where the time goes:
time: 1020 us
  waiting for transfers between devices  658 us (65%)
  matrix products  157 us (15%)
  blocking collectives  125 us (12%)
  local copies, waits for them, and re-layouts  35.4 us (3%)
  other arithmetic  28.5 us (3%)
  between operations  14.8 us (1%)
    reduce_scatter x1, waiting for transfers between devices, body(): lax.psum_scatter(grad_down, ('dp', 'fsdp'), scatter_dimension=0, tiled=True)  188 us
    reduce_scatter x1, waiting for transfers between devices, body(): lax.psum_scatter(grad_up, ('dp', 'fsdp'), scatter_dimension=0, tiled=True)  185 us
    unnamed x9, waiting for transfers between devices  157 us
    unnamed x2, blocking collectives  83.6 us
    all_gather x1, waiting for transfers between devices, body(): lax.all_gather(w_up, ('dp', 'fsdp'), axis=0, tiled=True)  74.9 us
    all_gather x1, waiting for transfers between devices, body(): lax.all_gather(w_down, ('dp', 'fsdp'), axis=0, tiled=True)  50.7 us
    all_gather x1, blocking collectives, body(): lax.all_gather(b_up, ('dp', 'fsdp'), axis=0, tiled=True)  41 us
    dot_general x4, matrix products, back_dot(): lax.dot_general(left, right, (((1,), (1,)), ((), ())), preferred_element_...  35.5 us
  transfers between devices with their start and end apart: 8, of which 6 were waited for; matrix products, arithmetic and copies ran while one was open for 17% of the time, Pallas kernels for 0%

commit v1 on v0

--- a/solution.py
+++ b/solution.py
@@ -1,6 +1,8 @@
 import jax
 import jax.numpy as jnp
 from jax import lax
+from jax.experimental import pallas as pl
+from jax.experimental.pallas import tpu as pltpu
 from jax.sharding import PartitionSpec as P
 
 HEADS = 16
@@ -273,6 +275,682 @@
     )
 
 
+BF = jnp.bfloat16
+F32 = jnp.float32
+MESH = pl.DeviceIdType.MESH
+SPAN = 256
+CW = 512
+NP, NA, NB, NC, ND = 4, 4, 5, 5, 3
+LANES = 128
+
+
+def nn(left, right):
+    return lax.dot_general(left, right, (((1,), (0,)), ((), ())), preferred_element_type=F32)
+
+
+def nt(left, right):
+    return lax.dot_general(left, right, (((1,), (1,)), ((), ())), preferred_element_type=F32)
+
+
+def loop(count, step):
+    def run(index, carry):
+        step(index)
+        return carry
+
+    lax.fori_loop(0, count, run, 0)
+
+
+def ds(start, size):
+    if isinstance(start, int):
+        return pl.ds(start, size)
+    return pl.ds(pl.multiple_of(start, size), size)
+
+
+def wait_for(region, sem):
+    pltpu.make_async_copy(region, region, sem).wait()
+
+
+class Place:
+    def __init__(self):
+        dp, fs = lax.axis_index("dp"), lax.axis_index("fsdp")
+        self.z, self.x = dp // 2, dp % 2
+        self.y, self.c = fs // 2, fs % 2
+
+    def device(self, z=None, x=None, y=None, c=None):
+        z = self.z if z is None else z
+        x = self.x if x is None else x
+        y = self.y if y is None else y
+        c = self.c if c is None else c
+        return (z * 2 + x, y * 2 + c)
+
+    def setup(self):
+        z, x, y, c = self.z, self.x, self.y, self.c
+        self.x1, self.y1 = x + (1 - c) * (1 - 2 * x), y + c * (1 - 2 * y)
+        self.x2, self.y2 = x + c * (1 - 2 * x), y + (1 - c) * (1 - 2 * y)
+        self.near = self.device(x=self.x1, y=self.y1)
+        self.far = self.device(x=self.x2, y=self.y2)
+        self.twin = self.device(c=1 - c)
+        self.ups = [self.device(z=(z + d) % 4) for d in (1, 2, 3)]
+        self.downs = [self.device(z=(z - d + 4) % 4) for d in (1, 2, 3)]
+
+    def slot(self, x, y):
+        return (x * 2 + y) * 2 + self.c
+
+
+def mega(
+    tokens, seg_row, seg_key, packed, cot_hbm, qkv_hbm, out_hbm, up_hbm, down_hbm,
+    lo_hbm, gt_hbm, g_qkv, g_out, g_up, g_down, g_small,
+    w_qkv, w_out, w_up, w_down, small, vec, up_bias, tok_t, q_s, k_s, v_s, prob, ctx, ctx_t, hat_s, r_s,
+    low, low_t, part, act_t, gelu_d, big, ra, rb, rc, rd, acc, bias_up_g, sg, sra, srb, src, srd,
+    ag_zr, ag_r1, ag_r2, ag_rc, ag_own, ag_s1, ag_s2,
+    sa_s, sa_r, sb_s, sb_r, sc_s, sc_r, sd_s, sd_r, sm_s, sm_r, loc,
+    cred_a, cred_b, cred_c, cred_d,
+):
+    at = Place()
+    at.setup()
+    z, x, y, c = at.z, at.x, at.y, at.c
+    rows, width = tokens.shape
+    ff = up_hbm.shape[1]
+    blocks = rows // SPAN
+    own, near_i, far_i, both_i = at.slot(x, y), at.slot(at.x1, at.y1), at.slot(at.x2, at.y2), at.slot(1 - x, 1 - y)
+
+    def send(src, dst, s, r, device):
+        pltpu.make_async_remote_copy(
+            src_ref=src, dst_ref=dst, send_sem=s, recv_sem=r, device_id=device, device_id_type=MESH
+        ).start()
+
+    pieces = [(packed, small, 0, LANES)]
+    for hbm, full, wide in ((qkv_hbm, w_qkv, 1024), (out_hbm, w_out, 1024), (up_hbm, w_up, 1024), (down_hbm, w_down, 256)):
+        for start in range(0, hbm.shape[1], wide):
+            pieces.append((hbm, full, start, wide))
+
+    def spot(k, lead):
+        _, full, start, wide = pieces[k]
+        return full.at[lead[0], lead[1], :, pl.ds(start, wide)]
+
+    every = slice(None)
+    barrier = pltpu.get_barrier_semaphore()
+    for peer in [at.near, at.far, at.twin] + at.ups:
+        pl.semaphore_signal(barrier, inc=1, device_id=peer, device_id_type=MESH)
+    pl.semaphore_wait(barrier, 6)
+
+    def gather_z(k):
+        hbm, full, start, wide = pieces[k]
+        source = hbm.at[:, pl.ds(start, wide)]
+        for peer in at.ups:
+            send(source, full.at[z, own, :, pl.ds(start, wide)], ag_s1.at[k], ag_zr.at[k], peer)
+        pltpu.make_async_copy(source, full.at[z, own, :, pl.ds(start, wide)], ag_own.at[k]).start()
+
+    def pass_on(k, index, peers):
+        block = spot(k, (every, index))
+        for peer, sem_s, sem_r in peers:
+            send(block, block, sem_s.at[k], sem_r.at[k], peer)
+
+    twin = (at.twin, ag_s2, ag_rc)
+    to_far = (at.far, ag_s1, ag_r2)
+    to_near = (at.near, ag_s1, ag_r1)
+
+    def gather_2(k):
+        wait_for(spot(k, (0, own)), ag_own.at[k])
+        wait_for(spot(k, (slice(0, 3), own)), ag_zr.at[k])
+        pass_on(k, own, [to_near, to_far, twin])
+
+    def gather_3(k):
+        wait_for(spot(k, (every, near_i)), ag_r1.at[k])
+        pass_on(k, near_i, [to_far, twin])
+
+    def gather_4(k):
+        wait_for(spot(k, (every, slice(0, 2))), ag_r2.at[k])
+        pass_on(k, far_i, [twin])
+        pass_on(k, both_i, [twin])
+
+    def gather_5(k):
+        wait_for(spot(k, (every, slice(0, 4))), ag_rc.at[k])
+
+    def gather_end(k):
+        wait_for(spot(k, (slice(0, 3), slice(0, 5))), ag_s1.at[k])
+        wait_for(spot(k, (every, slice(0, 4))), ag_s2.at[k])
+
+    keep = [c * (x * 2 + t) + (1 - c) * (t * 2 + y) for t in (0, 1)]
+    away = [c * ((1 - x) * 2 + t) + (1 - c) * (t * 2 + 1 - y) for t in (0, 1)]
+    mine = (1 - c) * x + c * y
+    total = 24
+
+    def send_a(k):
+        p, a = k % NP, k % NA
+        if k >= NA:
+            pl.semaphore_wait(cred_a, 1)
+        for plane in range(4):
+            send(part.at[p, plane, :, 1 - c], ra.at[a, plane], sa_s.at[p], sa_r.at[a], at.twin)
+
+    def add_a(k):
+        p, a = k % NP, k % NA
+        wait_for(ra.at[a], sa_r.at[a])
+
+        def step(plane):
+            mix = ra[a, plane].astype(F32) + part[p, plane, :, c].astype(F32)
+            ra[a, plane] = mix.astype(BF)
+
+        loop(4, step)
+        wait_for(ra.at[a], sa_s.at[p])
+
+    def send_b(k):
+        a, b = k % NA, k % NB
+        if k >= NB:
+            pl.semaphore_wait(cred_b, 1)
+        for t in (0, 1):
+            send(ra.at[a, :, away[t]], rb.at[b, :, t], sb_s.at[a], sb_r.at[b], at.far)
+
+    def add_b(k):
+        a, b = k % NA, k % NB
+        wait_for(rb.at[b], sb_r.at[b])
+
+        def step(plane):
+            for t in (0, 1):
+                mix = rb[b, plane, t].astype(F32) + ra[a, plane, keep[t]].astype(F32)
+                rb[b, plane, t] = mix.astype(BF)
+
+        loop(4, step)
+        wait_for(rb.at[b], sb_s.at[a])
+        if k + NA < total:
+            pl.semaphore_signal(cred_a, inc=1, device_id=at.twin, device_id_type=MESH)
+
+    def send_c(k):
+        b, cc = k % NB, k % NC
+        if k >= NC:
+            pl.semaphore_wait(cred_c, 1)
+        send(rb.at[b, :, 1 - mine], rc.at[cc], sc_s.at[b], sc_r.at[cc], at.near)
+
+    def add_c(k):
+        b, cc = k % NB, k % NC
+        wait_for(rc.at[cc], sc_r.at[cc])
+
+        def step(plane):
+            mix = rc[cc, plane].astype(F32) + rb[b, plane, mine].astype(F32)
+            rc[cc, plane] = mix.astype(BF)
+
+        loop(4, step)
+        wait_for(rc.at[cc], sc_s.at[b])
+        if k + NB < total:
+            pl.semaphore_signal(cred_b, inc=1, device_id=at.far, device_id_type=MESH)
+
+    def send_d(k):
+        cc, d = k % NC, k % ND
+        for o in range(3):
+            if k >= ND:
+                pl.semaphore_wait(cred_d.at[o], 1)
+            send(rc.at[cc, (z + o + 1) % 4], rd.at[d, o], sd_s.at[cc], sd_r.at[d], at.ups[o])
+
+    def target(k):
+        if k < 8:
+            return g_down.at[pl.ds(32 * (k // 2), 32), pl.ds(CW * (k % 2), CW)]
+        if k < 16:
+            return g_up.at[:, pl.ds(CW * (k - 8), CW)]
+        if k < 18:
+            return g_out.at[:, pl.ds(CW * (k - 16), CW)]
+        return g_qkv.at[:, pl.ds(CW * (k - 18), CW)]
+
+    def add_d(k):
+        cc, d = k % NC, k % ND
+        wait_for(rd.at[d], sd_r.at[d])
+        mix = rc[cc, z].astype(F32) + rd[d, 0].astype(F32) + rd[d, 1].astype(F32) + rd[d, 2].astype(F32)
+        target(k)[...] = mix
+        wait_for(rd.at[d], sd_s.at[cc])
+        if k + NC < total:
+            pl.semaphore_signal(cred_c, inc=1, device_id=at.near, device_id_type=MESH)
+        if k + ND < total:
+            for o in range(3):
+                pl.semaphore_signal(cred_d.at[o], inc=1, device_id=at.downs[o], device_id_type=MESH)
+
+    def advance(s):
+        adds = [(add_d, s - 7), (add_c, s - 5), (add_b, s - 3), (add_a, s - 1)]
+        sends = [(send_d, s - 5), (send_c, s - 3), (send_b, s - 1), (send_a, s)]
+        for op, k in adds:
+            if 0 <= k < total:
+                op(k)
+        for op, k in sends:
+            if 0 <= k < total:
+                op(k)
+
+    def flat(ref, n):
+        return ref[:, :, :, ds(n, SPAN)].reshape(width, SPAN)
+
+    def transpose_rows(src, dst):
+        def step(n):
+            dst[ds(n * SPAN, SPAN), :] = src[:, ds(n * SPAN, SPAN)].T
+
+        loop(width // SPAN, step)
+
+    def project(which, dst, row):
+        def step(n):
+            cols = ds(n * SPAN, SPAN)
+            value = nn(tokens[...], flat(w_qkv, which * width + n * SPAN))
+            if row is not None:
+                value = value + vec[row:row + 1, cols]
+            dst[:, cols] = value.astype(BF)
+
+        loop(width // SPAN, step)
+
+    heads_wide = LANES // 2
+
+    def split(value, high):
+        lane = lax.broadcasted_iota(jnp.int32, value.shape, 1)
+        return jnp.where((lane >= heads_wide) if high else (lane < heads_wide), value, jnp.zeros_like(value))
+
+    scale = float(heads_wide) ** (-0.5)
+    pairs = width // LANES
+
+    def attend(unit):
+        block, pair = unit // pairs, unit % pairs
+        r, l = ds(block * SPAN, SPAN), ds(pair * LANES, LANES)
+        queries, key_rows, values_t = q_s[r, l], k_s[r, l], v_s[r, l].T
+        diagonal = lax.broadcasted_iota(jnp.int32, (SPAN, SPAN), 0) == lax.broadcasted_iota(jnp.int32, (SPAN, SPAN), 1)
+        allowed = (seg_key[r, :] == seg_row[:, r]) | diagonal
+        halves = []
+        for high in (0, 1):
+            scores = nt(split(key_rows, high), queries) * scale
+            scores = jnp.where(allowed, scores, NEG_FILL)
+            raised = jnp.exp(scores - jnp.max(scores, 0, keepdims=True))
+            weights = (raised * (1.0 / jnp.sum(raised, 0, keepdims=True))).astype(BF)
+            prob[unit, high] = weights
+            halves.append(nn(values_t[heads_wide * high:heads_wide * (high + 1), :], weights))
+        joined = jnp.concatenate(halves, 0).astype(BF)
+        ctx_t[l, r] = joined
+        ctx[r, l] = joined.T
+
+    def attend_back(unit):
+        block, pair = unit // pairs, unit % pairs
+        r, l = ds(block * SPAN, SPAN), ds(pair * LANES, LANES)
+        queries, key_rows, values, grads = q_s[r, l], k_s[r, l], v_s[r, l], ctx[r, l]
+        keys_t = key_rows.T
+        value_grad = jnp.zeros((SPAN, LANES), F32)
+        key_grad = jnp.zeros((SPAN, LANES), F32)
+        halves = []
+        for high in (0, 1):
+            weights = prob[unit, high]
+            value_grad = value_grad + nn(weights, split(grads, high))
+            wide = weights.astype(F32)
+            prob_grad = nt(split(values, high), grads)
+            inner = jnp.sum(wide * prob_grad, 0, keepdims=True)
+            score_grad = (wide * (prob_grad - inner)).astype(BF)
+            key_grad = key_grad + nn(score_grad, split(queries, high))
+            halves.append(nn(keys_t[heads_wide * high:heads_wide * (high + 1), :], score_grad))
+        q_s[r, l] = (jnp.concatenate(halves, 0) * scale).T.astype(BF)
+        k_s[r, l] = (key_grad * scale).astype(BF)
+        v_s[r, l] = value_grad.astype(BF)
+
+    ROWS = 64
+
+    def folded(value):
+        return jnp.sum(value.reshape(ROWS // 8, 8, width), 0)
+
+    def norm_stats(hidden):
+        center = hidden - jnp.mean(hidden, -1, keepdims=True)
+        spread = jnp.mean(center * center, -1, keepdims=True)
+        r = lax.rsqrt(spread + EPSILON)
+        return center * r, r
+
+    def out_project():
+        def step(n):
+            cols = ds(n * SPAN, SPAN)
+            big[:, cols] = tokens[:, cols].astype(F32) + nn(ctx[...], flat(w_out, n * SPAN)) + vec[2:3, cols]
+
+        loop(width // SPAN, step)
+
+    def norm_one():
+        def step(n):
+            r = ds(n * ROWS, ROWS)
+            hat, inverse = norm_stats(big[r, :])
+            hat_s[r, :] = hat
+            r_s[r, :] = inverse
+            normed = hat * vec[3:4, :] + vec[4:5, :]
+            low[r, :] = normed.astype(BF)
+            big[r, :] = normed + vec[5:6, :]
+
+        loop(rows // ROWS, step)
+
+    def up_units(first, count):
+        def step(index):
+            u = first + index
+            cols = ds(u * SPAN, SPAN)
+            value = nn(low[...], flat(w_up, u * SPAN)) + up_bias[:, cols]
+            phi = 0.5 + 0.5 * lax.erf(value * (0.5 ** 0.5))
+            active = (value * phi).astype(BF)
+            slope = phi + value * (jnp.exp(-0.5 * value * value) * 0.3989422804014327)
+            gelu_d[:, cols] = slope.astype(BF)
+            act_t[ds(u * SPAN, SPAN), :] = active.T
+            wide = u // 2
+            part[wide // 2, ds((wide % 2) * 2, 2), :, :, :, ds((u % 2) * SPAN, SPAN)] = active.reshape(2, 4, 2, 32, SPAN)
+
+        loop(count, step)
+
+    def down_piece(piece):
+        cols = pl.ds(piece * SPAN, SPAN)
+
+        def step(wide):
+            slot, half = wide // 2, wide % 2
+            left = part[slot, ds(half * 2, 2)].reshape(rows, CW)
+            right = w_down[slot, ds(half * 4, 4), :, cols].reshape(CW, SPAN)
+            big[:, cols] += nn(left, right)
+
+        loop(ff // CW, step)
+
+    def norm_two():
+        for row in range(6):
+            acc[row] = jnp.zeros((8, width), F32)
+
+        def step(n):
+            r = ds(n * ROWS, ROWS)
+            hat, inverse = norm_stats(big[r, :])
+            ctx[r, :] = (hat * vec[6:7, :] + vec[7:8, :]).astype(BF)
+            cot = low[r, :].astype(F32)
+            acc[0] += folded(cot * hat)
+            acc[1] += folded(cot)
+            scaled = cot * vec[6:7, :]
+            grad = inverse * (
+                scaled - jnp.mean(scaled, -1, keepdims=True) - hat * jnp.mean(scaled * hat, -1, keepdims=True)
+            )
+            big[r, :] = grad
+            rounded = grad.astype(BF)
+            low[r, :] = rounded
+            acc[2] += folded(rounded.astype(F32))
+
+        loop(rows // ROWS, step)
+
+    def norm_one_back():
+        def step(n):
+            r = ds(n * ROWS, ROWS)
+            incoming, hat = big[r, :], hat_s[r, :]
+            acc[3] += folded(incoming * hat)
+            acc[4] += folded(incoming)
+            scaled = incoming * vec[3:4, :]
+            grad = r_s[r, :] * (
+                scaled - jnp.mean(scaled, -1, keepdims=True) - hat * jnp.mean(scaled * hat, -1, keepdims=True)
+            )
+            big[r, :] = grad
+            rounded = grad.astype(BF)
+            low[r, :] = rounded
+            acc[5] += folded(rounded.astype(F32))
+
+        loop(rows // ROWS, step)
+
+    def put_part(k, left, right):
+        slot = k % NP
+
+        def step(n):
+            cols = ds(n * SPAN, SPAN)
+            part[slot, :, :, :, :, cols] = nn(left(), right(n)).astype(BF).reshape(4, 4, 2, 32, SPAN)
+
+        loop(CW // SPAN, step)
+
+    def produce(k):
+        if k < 8:
+            group, half = k // 2, k % 2
+            put_part(
+                k,
+                lambda: act_t[...].reshape(32, 128, rows)[:, 32 * group:32 * group + 32].reshape(width, rows),
+                lambda n: low[:, ds(half * CW + n * SPAN, SPAN)],
+            )
+        elif k < 16:
+            put_part(k, lambda: low_t[...], lambda n: gelu_d[:, ds((k - 8) * CW + n * SPAN, SPAN)])
+        elif k < 18:
+            put_part(k, lambda: ctx_t[...], lambda n: low[:, ds((k - 16) * CW + n * SPAN, SPAN)])
+        else:
+            ref = (q_s, k_s, v_s)[(k - 18) // 2]
+            put_part(k, lambda: tok_t[...], lambda n: ref[:, ds((k % 2) * CW + n * SPAN, SPAN)])
+
+    def up_back(first, count):
+        def step(index):
+            u = first + index
+            cols = ds(u * SPAN, SPAN)
+            weight = w_down[u // 4, ds((u % 4) * 2, 2)].reshape(SPAN, width)
+            grad = (nt(low[...], weight) * gelu_d[:, cols].astype(F32)).astype(BF)
+            gelu_d[:, cols] = grad
+            bias_up_g[:, cols] = jnp.sum(grad.astype(F32), 0, keepdims=True)
+
+        loop(count, step)
+
+    def normed_back(plane):
+        cols = pl.ds(plane * SPAN, SPAN)
+        big[:, cols] += nt(gelu_d[...], w_up[plane].reshape(SPAN, ff))
+
+    def context_back():
+        def step(plane):
+            ctx[:, ds(plane * SPAN, SPAN)] = nt(low[...], w_out[plane].reshape(SPAN, width)).astype(BF)
+
+        loop(4, step)
+
+    def token_back(plane):
+        cols = pl.ds(plane * SPAN, SPAN)
+        weight = w_qkv[plane].reshape(SPAN, 3 * width)
+        total_grad = nt(q_s[...], weight[:, :width]) + nt(k_s[...], weight[:, width:2 * width])
+        big[:, cols] += total_grad + nt(v_s[...], weight[:, 2 * width:])
+
+    count = len(pieces)
+    for k in range(count):
+        gather_z(k)
+    gather_2(0)
+    gather_2(1)
+    gather_3(0)
+    gather_4(0)
+    gather_2(2)
+    gather_5(0)
+    for g in range(8):
+        tile = small[g // 2, 4 * (g % 2)].astype(F32)
+        for j in range(1, 4):
+            tile = tile + small[g // 2, 4 * (g % 2) + j].astype(F32)
+        vec[:, LANES * g:LANES * (g + 1)] = tile[0:8]
+    for j in range(32):
+        up_bias[:, LANES * j:LANES * (j + 1)] = small[j // 8, j % 8].astype(F32)[8:9]
+    transpose_rows(tokens, tok_t)
+
+    units = blocks * pairs
+    half = units // 2
+
+    def work(k):
+        if k <= 3:
+            project(k - 1, (q_s, k_s, v_s)[k - 1], (0, None, 1)[k - 1])
+            if k == 3:
+                loop(half, attend)
+        elif k == 4:
+            loop(units - half, lambda u: attend(u + half))
+            out_project()
+            norm_one()
+        elif k <= 8:
+            up_units(4 * (k - 5), 4)
+            if k == 8:
+                transpose_rows(low, low_t)
+                copy = pltpu.make_async_copy(cot_hbm, low, loc.at[0])
+                copy.start()
+        else:
+            down_piece(k - 9)
+
+    for tick in range(1, count + 2):
+        if tick + 2 < count:
+            gather_2(tick + 2)
+        if tick < count:
+            gather_3(tick)
+        if 1 <= tick - 1 < count:
+            gather_4(tick - 1)
+        if 1 <= tick - 2 < count:
+            gather_5(tick - 2)
+            work(tick - 2)
+
+    pltpu.make_async_copy(cot_hbm, low, loc.at[0]).wait()
+    norm_two()
+    pltpu.make_async_copy(ctx, lo_hbm, loc.at[1]).start()
+    others = {s: [] for s in range(total + 8)}
+    for s in range(4):
+        others[s].append(lambda s=s: up_back(4 * s, 4))
+        others[4 + s].append(lambda s=s: normed_back(s))
+    others[8].append(norm_one_back)
+    others[8].append(lambda: pltpu.make_async_copy(ctx, lo_hbm, loc.at[1]).wait())
+    others[8].append(context_back)
+    for s in range(8):
+        others[9 + s].append(lambda s=s: loop(2, lambda u: attend_back(u + 2 * s)))
+    for s in range(4):
+        others[18 + s].append(lambda s=s: token_back(s))
+    others[22].append(lambda: pltpu.make_async_copy(big, gt_hbm, loc.at[0]).start())
+
+    def small_grads():
+        for row in range(6):
+            acc[row, 0:1] = jnp.sum(acc[row], 0, keepdims=True)
+        for g in range(8):
+            cols = slice(LANES * g, LANES * (g + 1))
+            query_sum = jnp.sum(q_s[:, cols].astype(F32), 0, keepdims=True)
+            value_sum = jnp.sum(v_s[:, cols].astype(F32), 0, keepdims=True)
+            tile = jnp.concatenate(
+                [query_sum, value_sum] + [acc[row, 0:1, cols] for row in (5, 3, 4, 2, 0, 1)], 0
+            )
+            for j in range(4 * g, 4 * g + 4):
+                sg[j // 8, (j % 8) // 2, j % 2, 0:8] = tile
+                line = bias_up_g[:, LANES * j:LANES * (j + 1)]
+                sg[j // 8, (j % 8) // 2, j % 2, 8:16] = jnp.broadcast_to(line, (8, LANES))
+
+    def small_a():
+        for plane in range(4):
+            send(sg.at[plane, :, 1 - c], sra.at[plane], sm_s.at[0], sm_r.at[0], at.twin)
+
+    def small_b():
+        wait_for(sra, sm_r.at[0])
+        for plane in range(4):
+            sra[plane] += sg[plane, :, c]
+        for t in (0, 1):
+            send(sra.at[:, away[t]], srb.at[:, t], sm_s.at[1], sm_r.at[1], at.far)
+
+    def small_c():
+        wait_for(srb, sm_r.at[1])
+        for t in (0, 1):
+            srb[:, t] += sra[:, keep[t]]
+        send(srb.at[:, 1 - mine], src, sm_s.at[2], sm_r.at[2], at.near)
+
+    def small_d():
+        wait_for(src, sm_r.at[2])
+        src[...] += srb[:, mine]
+        for o in range(3):
+            send(src.at[(z + o + 1) % 4], srd.at[o], sm_s.at[3], sm_r.at[3], at.ups[o])
+
+    def small_e():
+        wait_for(srd, sm_r.at[3])
+        g_small[...] = src[z] + srd[0] + srd[1] + srd[2]
+        wait_for(sra, sm_s.at[0])
+        wait_for(srb, sm_s.at[1])
+        wait_for(src, sm_s.at[2])
+        wait_for(srd, sm_s.at[3])
+
+    others[17].append(small_grads)
+    for s, op in ((18, small_a), (19, small_b), (21, small_c), (23, small_d), (25, small_e)):
+        others[s].append(op)
+
+    for s in range(total + 7):
+        if s < total:
+            produce_now = s
+            for op in others[s]:
+                if s in (8,):
+                    op()
+            produce(produce_now)
+        advance(s)
+        for op in others[s]:
+            if s not in (8,):
+                op()
+
+    for k in range(count):
+        gather_end(k)
+    pltpu.make_async_copy(big, gt_hbm, loc.at[0]).wait()
+
+
+def fused(
+    tokens, segment_ids, pad_mask, cotangent, w_qkv, b_query, b_value, w_out, b_out, gain_attn, shift_attn,
+    w_up, b_up, w_down, b_down, gain_ffn, shift_ffn,
+):
+    rows, width = tokens.shape
+    ff = w_up.shape[1]
+    place = lax.axis_index("fsdp")
+    vectors = jnp.stack([b_query, b_value, b_out, gain_attn, shift_attn, b_down, gain_ffn, shift_ffn])
+    quarter = jnp.arange(4, dtype=jnp.int32)[None, :, None] == place
+    placed = jnp.where(quarter, vectors[:, None, :], jnp.zeros((), BF)).reshape(8, LANES)
+    packed = jnp.concatenate([placed, jnp.broadcast_to(b_up[None, :], (8, LANES))], 0)
+    seg_row = segment_ids.reshape(1, rows)
+    seg_key = jnp.where(pad_mask == 1, segment_ids, -1).reshape(rows, 1)
+    vmem = pl.BlockSpec(memory_space=pltpu.VMEM)
+    anyw = pl.BlockSpec(memory_space=pl.ANY)
+    pairs = width // LANES
+    blocks = rows // SPAN
+    count = 13
+    dma = pltpu.SemaphoreType.DMA
+    scratch = [
+        pltpu.VMEM((4, 8, 32, 3 * width), BF),
+        pltpu.VMEM((4, 8, 32, width), BF),
+        pltpu.VMEM((4, 8, 32, ff), BF),
+        pltpu.VMEM((4, 8, 128, width), BF),
+        pltpu.VMEM((4, 8, 16, LANES), BF),
+        pltpu.VMEM((8, width), F32),
+        pltpu.VMEM((1, ff), F32),
+        pltpu.VMEM((width, rows), BF),
+        pltpu.VMEM((rows, width), BF),
+        pltpu.VMEM((rows, width), BF),
+        pltpu.VMEM((rows, width), BF),
+        pltpu.VMEM((blocks * pairs, 2, SPAN, SPAN), BF),
+        pltpu.VMEM((rows, width), BF),
+        pltpu.VMEM((width, rows), BF),
+        pltpu.VMEM((rows, width), F32),
+        pltpu.VMEM((rows, 1), F32),
+        pltpu.VMEM((rows, width), BF),
+        pltpu.VMEM((width, rows), BF),
+        pltpu.VMEM((NP, 4, 4, 2, 32, CW), BF),
+        pltpu.VMEM((ff, rows), BF),
+        pltpu.VMEM((rows, ff), BF),
+        pltpu.VMEM((rows, width), F32),
+        pltpu.VMEM((NA, 4, 4, 32, CW), BF),
+        pltpu.VMEM((NB, 4, 2, 32, CW), BF),
+        pltpu.VMEM((NC, 4, 32, CW), BF),
+        pltpu.VMEM((ND, 3, 32, CW), BF),
+        pltpu.VMEM((6, 8, width), F32),
+        pltpu.VMEM((1, ff), F32),
+        pltpu.VMEM((4, 4, 2, 16, LANES), F32),
+        pltpu.VMEM((4, 4, 16, LANES), F32),
+        pltpu.VMEM((4, 2, 16, LANES), F32),
+        pltpu.VMEM((4, 16, LANES), F32),
+        pltpu.VMEM((3, 16, LANES), F32),
+    ]
+    scratch += [dma((count,))] * 7
+    scratch += [
+        dma((NP,)), dma((NA,)), dma((NA,)), dma((NB,)), dma((NB,)), dma((NC,)), dma((NC,)), dma((ND,)),
+        dma((4,)), dma((4,)), dma((2,)),
+        pltpu.SemaphoreType.REGULAR, pltpu.SemaphoreType.REGULAR, pltpu.SemaphoreType.REGULAR,
+        pltpu.SemaphoreType.REGULAR((3,)),
+    ]
+    result, grad_tokens, g_qkv, g_out, g_up, g_down, g_small = pl.pallas_call(
+        mega,
+        out_shape=(
+            jax.ShapeDtypeStruct((rows, width), BF),
+            jax.ShapeDtypeStruct((rows, width), F32),
+            jax.ShapeDtypeStruct(w_qkv.shape, F32),
+            jax.ShapeDtypeStruct(w_out.shape, F32),
+            jax.ShapeDtypeStruct(w_up.shape, F32),
+            jax.ShapeDtypeStruct(w_down.shape, F32),
+            jax.ShapeDtypeStruct((16, LANES), F32),
+        ),
+        in_specs=[vmem] * 4 + [anyw] * 5,
+        out_specs=[anyw, anyw] + [vmem] * 5,
+        scratch_shapes=scratch,
+        compiler_params=pltpu.CompilerParams(
+            collective_id=0, has_side_effects=True, vmem_limit_bytes=67043328
+        ),
+        name="layer",
+    )(tokens, seg_row, seg_key, packed, cotangent, w_qkv, w_out, w_up, w_down)
+    own = lax.dynamic_slice(g_small, (0, place * 32), (8, 32))
+    return (
+        result, grad_tokens, g_qkv, own[0], own[1], g_out, own[2], own[3], own[4], g_up, g_small[8], g_down,
+        own[5], own[6], own[7],
+    )
+
+
+def layer(*arrays):
+    fast = lax.axis_size("dp") == 8 and lax.axis_size("fsdp") == 4
+    return fused(*arrays) if fast else body(*arrays)
+
+
 def solution(mesh):
     placed = (
         P(("dp", "fsdp"), None),
@@ -294,7 +972,7 @@
         P(("dp", "fsdp")),
     )
     return jax.shard_map(
-        body,
+        layer,
         mesh=mesh,
         in_specs=placed,
         out_specs=(

time: 1020 us -> 275 us (0.27)
  waiting for transfers between devices: 658 us -> 0 us
  Pallas kernels: 0 us -> 261 us
  matrix products: 157 us -> 0 us
  blocking collectives: 125 us -> 0 us
  other arithmetic: 28.5 us -> 1.31 us
  local copies, waits for them, and re-layouts: 35.4 us -> 11.8 us
  between operations: 14.8 us -> 0.69 us
    reduce_scatter x3 -> x0, waiting for transfers between devices: 373 us -> none  [the longest x1 188 us: body(): lax.psum_scatter(grad_down, ('dp', 'fsdp'), scatter_dimension=0, tiled=True)]
    pallas_call x0 -> x1, Pallas kernels: none -> 261 us  [fused(): pl.pallas_call(mega, out_shape=(jax.ShapeDtypeStruct((rows, width), BF),...]
    unnamed x9 -> x0, waiting for transfers between devices: 157 us -> none
    dot_general x18 -> x0, matrix products: 157 us -> none  [the longest x4 35.5 us: back_dot(): lax.dot_general(left, right, (((1,), (1,)), ((), ())), preferred_element_...]
    all_gather x4 -> x0, waiting for transfers between devices: 129 us -> none  [the longest x1 74.9 us: body(): lax.all_gather(w_up, ('dp', 'fsdp'), axis=0, tiled=True)]
    unnamed x2 -> x0, blocking collectives: 83.6 us -> none
    all_gather x1 -> x0, blocking collectives: 41 us -> none  [body(): lax.all_gather(b_up, ('dp', 'fsdp'), axis=0, tiled=True)]
    unnamed x56 -> x16, local copies, waits for them, and re-layouts: 29.1 us -> 6.59 us
  transfers between devices with their start and end apart: 8 -> 0, of which waited for: 6 -> 0; matrix products, arithmetic and copies ran while one was open for 17% -> 0% of each run, Pallas kernels for 0% -> 0%
where the time goes in v1:
time: 275 us; the launch traced here: 274 us
  Pallas kernels  261 us (95%)
  local copies, waits for them, and re-layouts  11.8 us (4%)
    pallas_call x1, Pallas kernels, fused(): pl.pallas_call(mega, out_shape=(jax.ShapeDtypeStruct((rows, width), BF),...  261 us
    unnamed x16, local copies, waits for them, and re-layouts  6.59 us

profile of v1, /device:TPU:0, one launch (start us, length us, event | category | flops | bytes accessed | tf_op | source)
XLA Modules:
  0.0 274.5 jit_solution(8679295724965573046)
XLA Ops:
  0.7 0.1 broadcast_in_dim.39
  0.7 0.1 broadcast_in_dim.40
  0.8 0.7 compare_select_fusion
  1.5 0.8 stack.35
  2.3 0.7 broadcast_in_dim.45
  3.0 0.1 broadcast_in_dim.43
  3.1 0.6 pad_maximum_fusion.packed
  3.7 0.9 copy.32.seg_key
  4.5 260.7 %layer.1 = (bf16[512,1024]{1,0:T(8,128)(2,1)}, f32[512,1024]{1,0:T(8,128)}, f32[32,3072]{1,0:T(8,128)}, f32[32,1024]{1,0:T(8,128)}, f32[32,4096]{1,0:T(8,128)}, /*index=5*/f32[128,1024]{1,0:T(8,128)}, f32[16,128]{1,0:T(8,128)}) custom-call(bf16[512,1024]{1,0:T(8,128)(2,1)} %tokens.1, s32[1,512]{1,0:T(1,128)} %bitcast.29, s32[512,1]{1,0:T(8,128)} %copy.32.seg_key, ...), custom_call_target="tpu_custom_call" | custom-call | tf_op jit(solution)/shard_map/layer/pallas_call | solution.py:923
  265.2 0.0 copy-start
  265.2 1.3 slice_bitcast_fusion.3
  266.6 0.8 constant_dynamic-slice_fusion
  267.3 0.5 slice_bitcast_fusion
  267.9 2.3 copy.39
  270.1 0.0 copy-done
  270.2 0.0 copy-start.3
  270.2 0.0 copy-start.4
  270.2 0.0 copy-start.2
  270.2 1.3 copy.40
  271.5 0.0 copy-done.3
  271.5 0.0 copy-start.1
  271.5 0.7 copy.41
  272.2 0.0 copy-done.4
  272.2 0.7 copy.42
  272.9 0.0 copy-done.2
  272.9 0.8 copy.43
  273.7 0.0 copy-done.1
  273.7 0.8 copy.44
  (3 shorter events, 0.0 us)
Async XLA Ops:
  265.2 4.9 %copy-start = (f32[512,1024]{1,0:T(8,128)S(1)}, f32[512,1024]{1,0:T(8,128)}, u32[]{:S(2)}) copy-start(f32[512,1024]{1,0:T(8,128)} %get-tuple-element.53) | copy-start | bytes 6291460
  270.2 1.3 copy-start.3
  270.2 2.1 copy-start.4
  270.2 2.7 copy-start.2
  271.5 2.2 copy-start.1
